TPU v7x, 256 devices: a whole 4x4x8 slice. The times are simulated.
256 devices in a mesh: pool: 8 (over z), tp: 32 (over x, y, core).
Axes of the slice: x: 4, y: 4, z: 8, core: 2. Of those that a mesh axis runs over, the one named last changes fastest.
Arguments:
- tokens: bfloat16 [4096, 8192], P(('pool', 'tp')), may hold values from -4 to 4
- lengths: int32 [8, 4], P('pool'), may hold values from 1 to 256, 512 in all within a row
- hit_pages: int32 [8, 4, 4], P('pool'), may hold values from 0 to 4095, as said below
- new_owner: int32 [8, 16], P('pool'), may hold values from 0 to 7, as said below
- w_query: bfloat16 [8192, 8192], P('pool', 'tp'), may hold values from -0.125 to 0.125
- w_keyval: bfloat16 [4096, 4096], P('pool', 'tp'), may hold values from -0.0625 to 0.0625
- w_out: bfloat16 [8192, 8192], P('tp', 'pool'), may hold values from -0.0625 to 0.0625
- pool_pages: bfloat16 [4096, 32, 2048], P('pool', 'tp'), may hold values from -65 to 65
Outputs:
- mixed: float32 [4096, 8192], P(('pool', 'tp'))
- new_store: bfloat16 [128, 32, 2048], P('pool', 'tp')
Inputs may be any that keep to these rules, and one draw needn't show every extreme that they name: Page p of the pool lies on pool index p // 512. In every group g at most 6 of the 16 entries of hit_pages[g] lie on one pool index, and some pool index holds exactly 6 of them in every group. A page may appear more than once. `new_owner`: in every group at most 2 of its 16 pages go to one pool index, and some pool index receives exactly 2 from every group. Row g holds the lengths of the 4 requests packed in group g, in order, and sums to 512.
All inputs are finite; a program needn't handle non-finite values.
Results may differ from a plain program's by a relative error of at most 0.009.
Values may be sent and summed in bfloat16 or wider, within the bound.
No kernel may reach another device: no remote copies, remote signals or barrier semaphores. Data moves between devices by JAX's collectives and lax.ppermute only.
A program may use at most 64 MiB of HBM per device.

v0:
```python
import math
import jax
import jax.numpy as jnp
from jax import lax
from jax.sharding import PartitionSpec as P

KVH = 8
HD = 128
PAGE = 32
REQS = 4
HITS = 4
CAPF = 6
CAPN = 2
EPSILON = 1e-06
ROPE_BASE = 1000000.0


def in_one_piece(arrays, axis, dim, along):
    ends, at = ([], 0)
    for a in arrays[:-1]:
        at += a.shape[along]
        ends.append(at)
    both = jnp.concatenate(arrays, axis=along)
    return tuple(jnp.split(lax.all_gather(both, axis, axis=dim, tiled=True), ends, axis=along))


def partner(value, axis, stride):
    mask = 2**stride
    pairs = [(source, source ^ mask) for source in range(lax.axis_size(axis))]
    return lax.ppermute(value, axis, pairs)


def rotate(values, positions):
    half = values.shape[-1] // 2
    steps_range = jnp.arange(half, dtype=jnp.float32)
    frequency = ROPE_BASE ** (-2.0 * steps_range / values.shape[-1])
    angles = positions.astype(jnp.float32)[:, None, None] * frequency[None, None, :]
    cosine = jnp.cos(angles)
    sine = jnp.sin(angles)
    first_half = values[..., :half]
    second_half = values[..., half:]
    return jnp.concatenate(
        [first_half * cosine - second_half * sine, second_half * cosine + first_half * sine],
        axis=-1,
    )


def slot_table(owners_row, capacity, seats):
    count_items = owners_row.shape[0]
    item_index = jnp.arange(count_items, dtype=jnp.int32)
    earlier_same = (owners_row[:, None] == owners_row[None, :]) & (
        item_index[None, :] < item_index[:, None]
    )
    slots = jnp.sum(earlier_same.astype(jnp.int32), axis=1)
    targets = owners_row * capacity + slots
    seat_index = jnp.arange(seats, dtype=jnp.int32)
    return targets[:, None] == seat_index[None, :]


def join_stack(held_new, held_cached, upper_half, other_new, other_cached):
    held_new = jnp.where(
        upper_half,
        jnp.concatenate([other_new, held_new], axis=0),
        jnp.concatenate([held_new, other_new], axis=0),
    )
    held_cached = jnp.where(
        upper_half,
        jnp.concatenate([other_cached, held_cached], axis=0),
        jnp.concatenate([held_cached, other_cached], axis=0),
    )
    return (held_new, held_cached)


def unstack_columns(held):
    return held.transpose(1, 0, 2).reshape(held.shape[1], held.shape[0] * held.shape[2])


def body(tokens, lengths, hit_pages, new_owner, w_query, w_keyval, w_out, pool_pages):
    rows_dev = tokens.shape[0]
    tp_count = lax.axis_size("tp")
    pool_count = lax.axis_size("pool")
    tp_rank = lax.axis_index("tp")
    group_rows = rows_dev * tp_count
    query_width = w_query.shape[1]
    part_width = w_keyval.shape[1] // 2
    heads_here = query_width // HD
    sharing = tp_count // KVH
    pages_here = pool_pages.shape[0]
    keyval_local = w_keyval.reshape(w_keyval.shape[0] * 2, part_width)
    pages_flat = pool_pages.reshape(pages_here, pool_pages.shape[1] * pool_pages.shape[2])
    tokens_wide = tokens.astype(jnp.float32)
    normed = (
        tokens_wide
        * lax.rsqrt(jnp.mean(tokens_wide * tokens_wide, axis=1, keepdims=True) + EPSILON)
    ).astype(jnp.bfloat16)
    full_query, full_keyval = in_one_piece((w_query, keyval_local), "pool", 0, 1)
    row_piece = lax.all_gather(normed, "tp", axis=0, tiled=True)
    projected = jnp.concatenate(
        [
            jnp.dot(row_piece, full_query, preferred_element_type=jnp.float32),
            jnp.dot(row_piece, full_keyval, preferred_element_type=jnp.float32),
        ],
        axis=1,
    )
    lengths_row = lengths[0]
    ends_at = jnp.cumsum(lengths_row)
    starts_at = ends_at - lengths_row
    token_index = jnp.arange(group_rows, dtype=jnp.int32)
    request_ids = jnp.sum((token_index[:, None] >= ends_at[None, :]).astype(jnp.int32), axis=1)
    chosen = request_ids[:, None] == jnp.arange(REQS, dtype=jnp.int32)[None, :]
    start_of = jnp.sum(jnp.where(chosen, starts_at[None, :], 0), axis=1)
    positions = token_index - start_of + HITS * PAGE
    queries = rotate(
        projected[:, :query_width].reshape(group_rows, heads_here, HD), positions
    ).astype(jnp.bfloat16)
    keyval_part = projected[:, query_width:].astype(jnp.bfloat16)
    page_ids = hit_pages.reshape(-1)
    count_hits = page_ids.shape[0]
    placed_hits = slot_table(page_ids // pages_here, CAPF, pool_count * CAPF)
    wanted = jnp.sum(jnp.where(placed_hits, (page_ids % pages_here)[:, None], 0), axis=0)
    wanted = wanted.reshape(pool_count, CAPF)
    asked = lax.all_to_all(wanted, "pool", split_axis=0, concat_axis=0, tiled=True)
    found = jnp.take(pages_flat, asked.reshape(-1), axis=0)
    found = found.reshape(asked.shape[0], asked.shape[1], pages_flat.shape[1])
    returned = lax.all_to_all(found, "pool", split_axis=0, concat_axis=0, tiled=True)
    returned = returned.reshape(pool_count * CAPF, PAGE * part_width)
    cached_part = jnp.dot(
        placed_hits.astype(jnp.bfloat16), returned, preferred_element_type=jnp.float32
    ).astype(jnp.bfloat16)
    cached_part = cached_part.reshape(count_hits * PAGE, part_width)
    bit_count = sharing.bit_length() - 1
    held_new = keyval_part[None]
    held_cached = cached_part[None]
    for bit_number in range(bit_count):
        other_new, other_cached = partner((held_new, held_cached), "tp", bit_number)
        upper_half = tp_rank // 2**bit_number % 2 == 1
        held_new, held_cached = join_stack(
            held_new, held_cached, upper_half, other_new, other_cached
        )
    new_head = unstack_columns(held_new)
    cached_head = unstack_columns(held_cached)
    new_keys = (
        rotate(new_head[:, :HD].astype(jnp.float32).reshape(group_rows, 1, HD), positions)
        .astype(jnp.bfloat16)
        .reshape(group_rows, HD)
    )
    stored_head = jnp.concatenate([new_keys, new_head[:, HD:]], axis=1)
    own_columns = lax.dynamic_slice_in_dim(
        stored_head, tp_rank % sharing * part_width, part_width, 1
    )
    page_count = group_rows // PAGE
    page_rows = own_columns.reshape(page_count, PAGE * part_width)
    placed_new = slot_table(new_owner[0], CAPN, pool_count * CAPN).astype(jnp.bfloat16)
    outgoing = jnp.dot(placed_new.T, page_rows, preferred_element_type=jnp.float32).astype(
        jnp.bfloat16
    )
    outgoing = outgoing.reshape(pool_count, CAPN, PAGE * part_width)
    new_store = lax.all_to_all(outgoing, "pool", split_axis=0, concat_axis=0, tiled=True).reshape(
        pool_count * CAPN, 1, PAGE * part_width
    )
    keys_all = jnp.concatenate([cached_head[:, :HD], new_keys], axis=0)
    values_all = jnp.concatenate([cached_head[:, HD:], new_head[:, HD:]], axis=0)
    cached_rows = count_hits * PAGE
    key_request = jnp.concatenate(
        [jnp.arange(cached_rows, dtype=jnp.int32) // (HITS * PAGE), request_ids]
    )
    key_order = jnp.concatenate([jnp.full((cached_rows,), -1, jnp.int32), token_index])
    block_rows = min(group_rows, 512)

    def attend(first_row):
        scores = jnp.einsum(
            "bhd,kd->hbk", queries, keys_all, preferred_element_type=jnp.float32
        ) / math.sqrt(HD)
        visible = (request_ids[:, None] == key_request[None, :]) & (
            key_order[None, :] <= token_index[:, None]
        )
        scores = jnp.where(visible[None], scores, -jnp.inf)
        highest = jnp.max(scores, axis=-1, keepdims=True)
        expanded = jnp.exp(scores - highest)
        weights = (expanded / jnp.sum(expanded, axis=-1, keepdims=True)).astype(jnp.bfloat16)
        blended = jnp.einsum(
            "hbk,kd->bhd", weights, values_all, preferred_element_type=jnp.float32
        ).astype(jnp.bfloat16)
        return blended.reshape(block_rows, query_width)

    attended = lax.map(
        attend, jnp.arange(group_rows // block_rows, dtype=jnp.int32) * block_rows
    ).reshape(group_rows, query_width)
    full_out = lax.all_gather(w_out, "pool", axis=1, tiled=True)
    summed = lax.psum_scatter(
        jnp.dot(attended, full_out, preferred_element_type=jnp.float32).astype(jnp.bfloat16),
        "tp",
        scatter_dimension=0,
        tiled=True,
    ).astype(jnp.float32)
    mixed = tokens_wide + summed
    return (mixed, new_store)


def solution(mesh):
    return jax.shard_map(
        body,
        mesh=mesh,
        in_specs=(
            P(("pool", "tp"), None),
            P("pool", None),
            P("pool", None, None),
            P("pool", None),
            P("pool", "tp"),
            P("pool", "tp"),
            P("tp", "pool"),
            P("pool", "tp", None),
        ),
        out_specs=(P(("pool", "tp"), None), P("pool", "tp", None)),
        check_vma=False,
    )
```

profile of v0, /device:TPU:2, one launch (start us, length us, event | category | flops | bytes accessed | tf_op | source)
XLA Modules:
  0.0 323.8 jit_solution(13723968068413563517)
XLA Ops:
  7.3 1.2 reshape.404
  8.4 2.0 pad_maximum_fusion
  10.6 1.1 fusion.18
  11.7 1.8 fusion.19
  13.6 0.7 all-gather.8.cloned.1.call-update
  15.3 8.5 %all-to-all-start = ((s32[8,1,6]{2,1,0:T(1,128)}), s32[8,1,6]{2,1,0:T(1,128)S(1)}, u32[]{:S(2)}, u32[]{:S(2)}) async-start(s32[8,1,6]{2,1,0:T(1,128)} %bitcast), calls=%async_computation | async-start | bytes 8192 | tf_op jit(solution)/shard_map/all_to_all | solution.py:122
  24.2 7.4 %all-to-all-done = s32[8,1,6]{2,1,0:T(1,128)S(1)} async-done(((s32[8,1,6]{2,1,0:T(1,128)}), s32[8,1,6]{2,1,0:T(1,128)S(1)}, u32[]{:S(2)}, u32[]{:S(2)}) %all-to-all-start) | async-done | bytes 224 | tf_op jit(solution)/shard_map/all_to_all | solution.py:122
  32.8 0.7 gather_fusion
  33.6 0.8 broadcast_select_fusion
  34.4 3.4 %all-to-all-start.1 = ((bf16[8,6,2048]{2,1,0:T(8,128)(2,1)}), bf16[8,6,2048]{2,1,0:T(8,128)(2,1)S(1)}, u32[]{:S(2)}, u32[]{:S(2)}) async-start(bf16[8,6,2048]{2,1,0:T(8,128)(2,1)} %broadcast_select_fusion), calls=%async_computation.1 | async-start | bytes 524288 | tf_op jit(solution)/shard_map/all_to_all | solution.py:125
  37.9 1.5 fusion.8
  39.4 13.0 %all-to-all-done.1 = bf16[8,6,2048]{2,1,0:T(8,128)(2,1)S(1)} async-done(((bf16[8,6,2048]{2,1,0:T(8,128)(2,1)}), bf16[8,6,2048]{2,1,0:T(8,128)(2,1)S(1)}, u32[]{:S(2)}, u32[]{:S(2)}) %all-to-all-start.1) | async-done | bytes 196640 | tf_op jit(solution)/shard_map/all_to_all | solution.py:125
  53.1 1.2 collective-permute-done
  54.3 1.7 collective-permute-start.1
  56.0 1.8 multiply_cosine_fusion
  57.8 2.2 collective-permute-done.1
  60.0 0.7 maximum_select_fusion
  60.7 33.0 %all-gather.6.cloned.1.call-done = bf16[8192,320]{1,0:T(8,128)(2,1)} async-done(((bf16[1024,320]{1,0:T(8,128)(2,1)}), bf16[8192,320]{1,0:T(8,128)(2,1)}) %all-gather.6.cloned.1.call-update) | async-done | bytes 5242896 | tf_op jit(solution)/shard_map/all_gather | solution.py:24
  93.7 59.0 %all-gather.4.cloned.1.call-done = bf16[512,8192]{1,0:T(8,128)(2,1)} async-done(((bf16[16,8192]{1,0:T(8,128)(2,1)}), bf16[512,8192]{1,0:T(8,128)(2,1)}) %all-gather.4.cloned.1.call-update) | async-done | bytes 8388624 | tf_op jit(solution)/shard_map/all_gather | solution.py:97
  152.7 6.8 %fusion.15 = bf16[1,512,64]{1,2,0:T(8,128)(2,1)S(1)} fusion(bf16[512,8192]{1,0:T(8,128)(2,1)} %all-gather.4.cloned.1.call-done, bf16[8192,320]{1,0:T(8,128)(2,1)} %all-gather.6.cloned.1.call-done), kind=kOutput, calls=%fused_computation.21 | convolution fusion | flops 536903680 | bytes 10551296 | tf_op jit(solution)/shard_map/dot_general | solution.py:101
  159.8 4.6 %fusion.1 = f32[512,256]{0,1:T(8,128)S(1)} fusion(bf16[512,8192]{1,0:T(8,128)(2,1)S(1)} %copy-done.1, bf16[8192,320]{1,0:T(8,128)(2,1)} %all-gather.6.cloned.1.call-done), kind=kOutput, calls=%fused_computation.3 | convolution fusion | flops 2147483648 | bytes 13107200 | tf_op jit(solution)/shard_map/dot_general | solution.py:100
  165.3 1.9 subtract_convert_fusion
  167.2 3.6 %collective-permute-done.3 = bf16[2,512,64]{1,2,0:T(8,128)(2,1)S(1)} collective-permute-done((bf16[2,512,64]{1,2,0:T(8,128)(2,1)S(1)}, bf16[2,512,64]{1,2,0:T(8,128)(2,1)S(1)}, u32[]{:S(2)}, u32[]{:S(2)}) %collective-permute-start.3) | collective-permute-done | bytes 131104 | tf_op jit(solution)/shard_map/ppermute | solution.py:30
  170.9 1.0 fusion.54
  172.1 1.2 fusion.33
  173.4 4.8 %fusion.56 = (f32[2,512]{1,0:T(2,128)S(1)}, f32[2,512,1024]{1,2,0:T(8,128)}) fusion(pred[512,1024]{0,1:T(8,128)(4,1)} %fusion.8, bf16[512,64]{1,0:T(8,128)(2,1)S(1)} %get-tuple-element.25, bf16[512,64]{1,0:T(8,128)(2,1)S(1)} %get-tuple-element.24, bf16[512,128]{1,0:T(8,128)(2,1)S(1)} %copy.56, bf16[512,2,64]{2,0,1:T(8,128)(2,1)} %get-tuple-element.21, ...), kind=kOutput, calls=%fused_computation.109 | convolution fusion | flops 273941504 | bytes 5246976 | tf_op jit(solution)/shard_map/while/body/eval_jaxpr/sub | solution.py:179
  178.2 2.7 fusion.11
  180.8 28.1 %all-gather.8.cloned.1.call-done = bf16[256,8192]{1,0:T(8,128)(2,1)} async-done(((bf16[256,1024]{1,0:T(8,128)(2,1)}), bf16[256,8192]{1,0:T(8,128)(2,1)}) %all-gather.8.cloned.1.call-update) | async-done | bytes 4194320 | tf_op jit(solution)/shard_map/all_gather | solution.py:189
  208.9 7.8 %convolution_convert_fusion = bf16[512,8192]{1,0:T(8,128)(2,1)} fusion(bf16[512,256]{0,1:T(8,128)(2,1)S(1)} %bitcast.70, bf16[256,8192]{1,0:T(8,128)(2,1)} %all-gather.8.cloned.1.call-done), kind=kOutput, calls=%fused_computation.2 | convolution fusion | flops 2151677952 | bytes 12845056 | tf_op jit(solution)/shard_map/dot_general | solution.py:191
  218.5 12.5 %all_to_all.19 = bf16[8,2,2048]{2,1,0:T(2,128)(2,1)S(1)} all-to-all(bf16[8,2,2048]{2,1,0:T(2,128)(2,1)S(1)} %reshape.413), channel_id=1, replica_groups=mesh['pool'=8,'tp'=32] {'pool'}, dimensions={0} | all-to-all | bytes 131072 | tf_op jit(solution)/shard_map/all_to_all | solution.py:158
  231.7 83.8 %reduce-scatter.2.cloned.1.call-done = bf16[16,8192]{1,0:T(8,128)(2,1)} async-done(((bf16[512,8192]{1,0:T(8,128)(2,1)}), bf16[16,8192]{1,0:T(8,128)(2,1)}) %reduce-scatter.2.cloned.1.call-update) | async-done | bytes 262160 | tf_op jit(solution)/shard_map/reduce_scatter | solution.py:190
  315.5 1.8 convert_add_fusion
  (70 shorter events, 7.6 us)
Async XLA Ops:
  7.2 25.6 %copy-start = (bf16[512,1,2048]{2,0,1:T(8,128)(2,1)S(1)}, bf16[512,1,2048]{2,0,1:T(8,128)(2,1)}, u32[]{:S(2)}) copy-start(bf16[512,1,2048]{2,0,1:T(8,128)(2,1)} %param.15) | copy-start | bytes 6291460
  7.2 30.7 %copy-start.3 = (s32[1024]{0:T(1024)S(1)}, s32[1024]{0:T(1024)}, u32[]{:S(2)}) copy-start(s32[1024]{0:T(1024)} %constant.140.clone.1) | copy-start | bytes 12292
  7.2 7.1 %copy-start.4 = (s32[1,4,4]{2,1,0:T(4,128)S(1)}, s32[1,4,4]{2,1,0:T(4,128)}, u32[]{:S(2)}) copy-start(s32[1,4,4]{2,1,0:T(4,128)} %param.10) | copy-start | bytes 196
  7.2 16.6 %copy-start.5 = (s32[1,4]{1,0:T(1,128)S(1)}, s32[1,4]{1,0:T(1,128)}, u32[]{:S(2)}) copy-start(s32[1,4]{1,0:T(1,128)} %param.9) | copy-start | bytes 52
  7.2 86.5 %all-gather.6.cloned.1.call-start = ((), (), s32[]{:S(2)}) async-start(), calls=%async_computation.5 | async-start | bytes 7077888 | tf_op jit(solution)/shard_map/all_gather | solution.py:24
  10.5 142.2 %all-gather.4.cloned.1.call-start = ((), (), s32[]{:S(2)}) async-start(), calls=%async_computation.4 | async-start | bytes 8650752 | tf_op jit(solution)/shard_map/all_gather | solution.py:97
  13.5 195.4 %all-gather.8.cloned.1.call-start = ((), (), s32[]{:S(2)}) async-start(), calls=%async_computation.6 | async-start | bytes 4718592 | tf_op jit(solution)/shard_map/all_gather | solution.py:189
  15.3 16.2 %all-to-all-start = ((s32[8,1,6]{2,1,0:T(1,128)}), s32[8,1,6]{2,1,0:T(1,128)S(1)}, u32[]{:S(2)}, u32[]{:S(2)}) async-start(s32[8,1,6]{2,1,0:T(1,128)} %bitcast), calls=%async_computation | async-start | bytes 8192 | tf_op jit(solution)/shard_map/all_to_all | solution.py:122
  34.4 18.0 %all-to-all-start.1 = ((bf16[8,6,2048]{2,1,0:T(8,128)(2,1)}), bf16[8,6,2048]{2,1,0:T(8,128)(2,1)S(1)}, u32[]{:S(2)}, u32[]{:S(2)}) async-start(bf16[8,6,2048]{2,1,0:T(8,128)(2,1)} %broadcast_select_fusion), calls=%async_computation.1 | async-start | bytes 524288 | tf_op jit(solution)/shard_map/all_to_all | solution.py:125
  37.8 277.7 %reduce-scatter.2.cloned.1.call-start = ((), (), s32[]{:S(2)}) async-start(), calls=%async_computation.7 | async-start | bytes 8650752 | tf_op jit(solution)/shard_map/reduce_scatter | solution.py:190
  53.0 1.3 collective-permute-start
  54.3 5.6 %collective-permute-start.1 = (bf16[2,512,64]{1,2,0:T(8,128)(2,1)S(1)}, bf16[2,512,64]{1,2,0:T(8,128)(2,1)S(1)}, u32[]{:S(2)}, u32[]{:S(2)}) collective-permute-start(bf16[2,512,64]{1,2,0:T(8,128)(2,1)S(1)} %maximum_select_fusion.2), channel_id=1, source_target_pairs={{0,2},{1,3},{2,0},{3,1},{4,6},{5,7},{6,4},{7,5},{8,10},{9,11},{10,... | collective-permute-start | bytes 393224 | tf_op jit(solution)/shard_map/ppermute | solution.py:30
  152.7 7.1 %copy-start.1 = (bf16[512,8192]{1,0:T(8,128)(2,1)S(1)}, bf16[512,8192]{1,0:T(8,128)(2,1)}, u32[]{:S(2)}) copy-start(bf16[512,8192]{1,0:T(8,128)(2,1)} %all-gather.4.cloned.1.call-done) | copy-start | bytes 25165828
  159.4 5.4 %collective-permute-start.2 = (bf16[1,512,64]{1,2,0:T(8,128)(2,1)S(1)}, bf16[1,512,64]{1,2,0:T(8,128)(2,1)S(1)}, u32[]{:S(2)}, u32[]{:S(2)}) collective-permute-start(bf16[1,512,64]{1,2,0:T(8,128)(2,1)S(1)} %fusion.15), channel_id=1, source_target_pairs={{0,1},{1,0},{2,3},{3,2},{4,5},{5,4},{6,7},{7,6},{8,9},{9,8},{10,11... | collective-permute-start | bytes 196616 | tf_op jit(solution)/shard_map/ppermute | solution.py:30
  164.9 5.9 %collective-permute-start.3 = (bf16[2,512,64]{1,2,0:T(8,128)(2,1)S(1)}, bf16[2,512,64]{1,2,0:T(8,128)(2,1)S(1)}, u32[]{:S(2)}, u32[]{:S(2)}) collective-permute-start(bf16[2,512,64]{1,2,0:T(8,128)(2,1)S(1)} %maximum_select_fusion.3), channel_id=1, source_target_pairs={{0,2},{1,3},{2,0},{3,1},{4,6},{5,7},{6,4},{7,5},{8,10},{9,11},{10,... | collective-permute-start | bytes 393224 | tf_op jit(solution)/shard_map/ppermute | solution.py:30
  216.7 0.7 copy-start.6
  216.7 98.8 %copy-start.2 = (bf16[16,8192]{1,0:T(8,128)(2,1)S(1)}, bf16[16,8192]{1,0:T(8,128)(2,1)}, u32[]{:S(2)}) copy-start(bf16[16,8192]{1,0:T(8,128)(2,1)} %param.8) | copy-start | bytes 786436
Sparse Core Ops, SparseCore 0:
  10.6 83.0 all-gather.5
  96.2 56.3 all-gather.3
  154.5 54.4 all-gather.7
  216.8 98.6 reduce-scatter.1
where the time goes:
time: 324 us
  waiting for transfers between devices  232 us (72%)
  matrix products  27.1 us (8%)
  other arithmetic  16.5 us (5%)
  starting transfers between devices  14.5 us (4%)
  between operations  14.1 us (4%)
  blocking collectives  12.5 us (4%)
  local copies, waits for them, and re-layouts  7.18 us (2%)
    reduce_scatter x1, waiting for transfers between devices, body(): lax.psum_scatter(jnp.dot(attended, full_out, preferred_element_type=jnp.f...  83.8 us
    all_gather x1, waiting for transfers between devices, body(): row_piece = lax.all_gather(normed, 'tp', axis=0, tiled=True)  59 us
    all_gather x1, waiting for transfers between devices, in_one_piece(): lax.all_gather(both, axis, axis=dim, tiled=True)  33 us
    all_gather x1, waiting for transfers between devices, body(): full_out = lax.all_gather(w_out, 'pool', axis=1, tiled=True)  28.1 us
    all_to_all x1, waiting for transfers between devices, body(): lax.all_to_all(found, 'pool', split_axis=0, concat_axis=0, tiled=True)  13 us
    all_to_all x1, blocking collectives, body(): lax.all_to_all(outgoing, 'pool', split_axis=0, concat_axis=0, tiled=True)  12.5 us
    all_to_all x1, starting transfers between devices, body(): lax.all_to_all(wanted, 'pool', split_axis=0, concat_axis=0, tiled=True)  8.47 us
    dot_general x1, matrix products, body(): jnp.dot(attended, full_out, preferred_element_type=jnp.float32)  7.77 us
  transfers between devices with their start and end apart: 10, of which 9 were waited for; matrix products, arithmetic and copies ran while one was open for 11% of the time, Pallas kernels for 0%

commit v1 on v0

--- a/solution.py
+++ b/solution.py
@@ -13,6 +13,18 @@
 CAPN = 2
 EPSILON = 1e-06
 ROPE_BASE = 1000000.0
+
+
+def post_the_trails(target):
+    return jnp.concatenate(
+        lax.all_to_all(
+            jnp.stack([target for _ in range(lax.axis_size("tp"))], axis=0),
+            axis_name="tp",
+            split_axis=0,
+            concat_axis=0,
+        ),
+        axis=0,
+    )
 
 
 def in_one_piece(arrays, axis, dim, along):
@@ -94,7 +106,7 @@
         * lax.rsqrt(jnp.mean(tokens_wide * tokens_wide, axis=1, keepdims=True) + EPSILON)
     ).astype(jnp.bfloat16)
     full_query, full_keyval = in_one_piece((w_query, keyval_local), "pool", 0, 1)
-    row_piece = lax.all_gather(normed, "tp", axis=0, tiled=True)
+    row_piece = post_the_trails(normed)
     projected = jnp.concatenate(
         [
             jnp.dot(row_piece, full_query, preferred_element_type=jnp.float32),

time: 324 us -> 333 us (1.028)
  starting transfers between devices: 14.5 us -> 34 us
  waiting for transfers between devices: 232 us -> 213 us
  local copies, waits for them, and re-layouts: 7.18 us -> 19.9 us
  other arithmetic: 16.5 us -> 11 us
    ppermute x4, waiting for transfers between devices: 7.03 us -> 95.4 us  [partner(): return lax.ppermute(value, axis, pairs)]
    all_gather x1 -> x0, waiting for transfers between devices: 59 us -> none  [body(): row_piece = lax.all_gather(normed, 'tp', axis=0, tiled=True)]
    all_gather x1, waiting for transfers between devices: 33 us -> 0.01 us  [in_one_piece(): lax.all_gather(both, axis, axis=dim, tiled=True)]
    all_gather x1, waiting for transfers between devices: 28.1 us -> 0.02 us  [body(): full_out = lax.all_gather(w_out, 'pool', axis=1, tiled=True)]
    ppermute x4, starting transfers between devices: 2.5 us -> 14.2 us  [partner(): return lax.ppermute(value, axis, pairs)]
    dot_general x0 -> x2, local copies, waits for them, and re-layouts: none -> 8.57 us  [body(): jnp.dot(row_piece, full_query, preferred_element_type=jnp.float32)]
    all_to_all x0 -> x1, starting transfers between devices: none -> 7.81 us  [post_the_trails(): lax.all_to_all(jnp.stack([target for _ in range(lax.axis_size('tp'))], ax...]
    all_to_all x0 -> x1, waiting for transfers between devices: none -> 7.14 us  [post_the_trails(): lax.all_to_all(jnp.stack([target for _ in range(lax.axis_size('tp'))], ax...]
  transfers between devices with their start and end apart: 10 -> 10, of which waited for: 9 -> 7; matrix products, arithmetic and copies ran while one was open for 11% -> 14% of each run, Pallas kernels for 0% -> 0%
where the time goes in v1:
time: 333 us; the launch traced here: 332 us
  waiting for transfers between devices  213 us (64%)
  starting transfers between devices  34 us (10%)
  matrix products  29.3 us (9%)
  local copies, waits for them, and re-layouts  19.9 us (6%)
  between operations  14.1 us (4%)
  other arithmetic  11 us (3%)
  blocking collectives  10.8 us (3%)
    ppermute x4, waiting for transfers between devices, partner(): return lax.ppermute(value, axis, pairs)  95.4 us
    reduce_scatter x1, waiting for transfers between devices, body(): lax.psum_scatter(jnp.dot(attended, full_out, preferred_element_type=jnp.f...  89.2 us
    all_to_all x1, waiting for transfers between devices, body(): lax.all_to_all(found, 'pool', split_axis=0, concat_axis=0, tiled=True)  14.5 us
    ppermute x4, starting transfers between devices, partner(): return lax.ppermute(value, axis, pairs)  14.2 us
    all_to_all x1, blocking collectives, body(): lax.all_to_all(outgoing, 'pool', split_axis=0, concat_axis=0, tiled=True)  10.8 us
    dot_general x2, local copies, waits for them, and re-layouts, body(): jnp.dot(row_piece, full_query, preferred_element_type=jnp.float32)  8.57 us
    all_to_all x1, starting transfers between devices, body(): lax.all_to_all(wanted, 'pool', split_axis=0, concat_axis=0, tiled=True)  8.47 us
    all_to_all x1, starting transfers between devices, post_the_trails(): lax.all_to_all(jnp.stack([target for _ in range(lax.axis_size('tp'))], ax...  7.81 us
  transfers between devices with their start and end apart: 10, of which 7 were waited for; matrix products, arithmetic and copies ran while one was open for 14% of the time, Pallas kernels for 0%

profile of v1, /device:TPU:2, one launch (start us, length us, event | category | flops | bytes accessed | tf_op | source)
XLA Modules:
  0.0 332.5 jit_solution(10483996847982490141)
XLA Ops:
  7.2 1.2 reshape.409
  8.4 2.0 pad_maximum_fusion
  10.5 0.8 reshape.402
  12.2 8.5 %all-to-all-start = ((s32[8,1,6]{2,1,0:T(1,128)}), s32[8,1,6]{2,1,0:T(1,128)S(1)}, u32[]{:S(2)}, u32[]{:S(2)}) async-start(s32[8,1,6]{2,1,0:T(1,128)} %bitcast), calls=%async_computation | async-start | bytes 8192 | tf_op jit(solution)/shard_map/all_to_all | solution.py:134
  20.7 1.1 fusion.16
  21.8 6.5 %all-to-all-done = s32[8,1,6]{2,1,0:T(1,128)S(1)} async-done(((s32[8,1,6]{2,1,0:T(1,128)}), s32[8,1,6]{2,1,0:T(1,128)S(1)}, u32[]{:S(2)}, u32[]{:S(2)}) %all-to-all-start) | async-done | bytes 224 | tf_op jit(solution)/shard_map/all_to_all | solution.py:134
  29.6 0.7 gather_fusion
  30.4 0.8 broadcast_select_fusion
  31.2 3.4 %all-to-all-start.1 = ((bf16[8,6,2048]{2,1,0:T(8,128)(2,1)}), bf16[8,6,2048]{2,1,0:T(8,128)(2,1)S(1)}, u32[]{:S(2)}, u32[]{:S(2)}) async-start(bf16[8,6,2048]{2,1,0:T(8,128)(2,1)} %broadcast_select_fusion), calls=%async_computation.1 | async-start | bytes 524288 | tf_op jit(solution)/shard_map/all_to_all | solution.py:137
  34.7 14.5 %all-to-all-done.1 = bf16[8,6,2048]{2,1,0:T(8,128)(2,1)S(1)} async-done(((bf16[8,6,2048]{2,1,0:T(8,128)(2,1)}), bf16[8,6,2048]{2,1,0:T(8,128)(2,1)S(1)}, u32[]{:S(2)}, u32[]{:S(2)}) %all-to-all-start.1) | async-done | bytes 196640 | tf_op jit(solution)/shard_map/all_to_all | solution.py:137
  49.2 4.2 %stack.2 = bf16[32,16,8192]{2,1,0:T(8,128)(2,1)} broadcast(bf16[16,8192]{1,0:T(8,128)(2,1)S(1)} %fusion.17), dimensions={1,2} | broadcast | bytes 8650752 | tf_op jit(solution)/shard_map/stack | solution.py:21
  53.5 7.8 %all-to-all-start.2 = ((bf16[32,16,8192]{2,1,0:T(8,128)(2,1)}), bf16[32,16,8192]{2,1,0:T(8,128)(2,1)}, u32[]{:S(2)}, u32[]{:S(2)}) async-start(bf16[32,16,8192]{2,1,0:T(8,128)(2,1)} %stack.2), calls=%async_computation.2 | async-start | bytes 16777216 | tf_op jit(solution)/shard_map/all_to_all | solution.py:20
  61.3 0.7 all-gather.5.cloned.1.call-update
  62.5 0.8 fusion.6
  64.2 1.1 collective-permute-done
  65.3 1.6 collective-permute-start.1
  67.4 91.3 %collective-permute-done.1 = bf16[2,512,64]{1,2,0:T(8,128)(2,1)S(1)} collective-permute-done((bf16[2,512,64]{1,2,0:T(8,128)(2,1)S(1)}, bf16[2,512,64]{1,2,0:T(8,128)(2,1)S(1)}, u32[]{:S(2)}, u32[]{:S(2)}) %collective-permute-start.1) | collective-permute-done | bytes 131104 | tf_op jit(solution)/shard_map/ppermute | solution.py:42
  158.8 7.1 %all-to-all-done.2 = bf16[32,16,8192]{2,1,0:T(8,128)(2,1)} async-done(((bf16[32,16,8192]{2,1,0:T(8,128)(2,1)}), bf16[32,16,8192]{2,1,0:T(8,128)(2,1)}, u32[]{:S(2)}, u32[]{:S(2)}) %all-to-all-start.2) | async-done | bytes 8388640 | tf_op jit(solution)/shard_map/all_to_all | solution.py:20
  165.9 6.8 %fusion.13 = bf16[1,512,64]{1,2,0:T(8,128)(2,1)S(1)} fusion(bf16[512,8192]{1,0:T(8,128)(2,1)} %bitcast.6, bf16[8192,320]{1,0:T(8,128)(2,1)} %all-gather.3.cloned.1.call-done), kind=kOutput, calls=%fused_computation.20 | convolution fusion | flops 536903680 | bytes 10551296 | tf_op jit(solution)/shard_map/dot_general | solution.py:113
  172.8 2.2 slice_bitcast_fusion
  175.0 6.3 %copy.49 = bf16[256,8192]{1,0:T(8,128)(2,1)} copy(bf16[256,8192]{0,1:T(8,128)(2,1)} %slice_bitcast_fusion) | data formatting | bytes 8388608 | tf_op jit(solution)/shard_map/dot_general | solution.py:112
  181.4 6.9 %fusion.54 = f32[512,2,128]{0,2,1:T(8,128)S(1)} fusion(bf16[512,8192,1]{1,0,2:T(8,128)(2,1)} %bitcast.22, bf16[2,128,8192]{2,1,0:T(8,128)(2,1)} %bitcast.71), kind=kOutput, calls=%fused_computation.108 | convolution fusion | flops 2147483648 | bytes 13107200 | tf_op jit(solution)/shard_map/dot_general | solution.py:112
  188.4 12.4 %collective-permute-start.3 = (bf16[2,512,64]{1,2,0:T(8,128)(2,1)S(1)}, bf16[2,512,64]{1,2,0:T(8,128)(2,1)S(1)}, u32[]{:S(2)}, u32[]{:S(2)}) collective-permute-start(bf16[2,512,64]{1,2,0:T(8,128)(2,1)S(1)} %maximum_select_fusion.3), channel_id=1, source_target_pairs={{0,2},{1,3},{2,0},{3,1},{4,6},{5,7},{6,4},{7,5},{8,10},{9,11},{10,... | collective-permute-start | bytes 393224 | tf_op jit(solution)/shard_map/ppermute | solution.py:42
  200.7 0.8 subtract_convert_fusion
  201.5 2.9 collective-permute-done.3
  205.4 1.2 fusion.32
  206.6 4.6 %fusion.53 = (f32[2,512]{1,0:T(2,128)S(1)}, f32[2,512,1024]{1,2,0:T(8,128)}) fusion(pred[512,1024]{0,1:T(8,128)(4,1)S(1)} %fusion.6, bf16[512,2,64]{0,2,1:T(8,128)(2,1)} %get-tuple-element.21, bf16[512,2,64]{0,2,1:T(8,128)(2,1)} %get-tuple-element.20, bf16[512,64]{1,0:T(8,128)(2,1)S(1)} %get-tuple-element.23, bf16[512,64]{1,0:T(8,128)(2,1)S(1)} %get-tuple-element.22, ...), kind=kOutput, calls=%fused_computation.107 | convolution fusion | flops 273941504 | bytes 5246976 | tf_op jit(solution)/shard_map/while/body/eval_jaxpr/sub | solution.py:191
  211.2 2.7 fusion.9
  214.0 7.8 %convolution_convert_fusion = bf16[512,8192]{1,0:T(8,128)(2,1)} fusion(bf16[512,256]{0,1:T(8,128)(2,1)S(1)} %bitcast.74, bf16[256,8192]{1,0:T(8,128)(2,1)} %all-gather.5.cloned.1.call-done), kind=kOutput, calls=%fused_computation.2 | convolution fusion | flops 2151677952 | bytes 12845056 | tf_op jit(solution)/shard_map/dot_general | solution.py:203
  223.6 10.8 %all_to_all.24 = bf16[8,2,2048]{2,1,0:T(2,128)(2,1)S(1)} all-to-all(bf16[8,2,2048]{2,1,0:T(2,128)(2,1)S(1)} %reshape.417), channel_id=1, replica_groups=mesh['pool'=8,'tp'=32] {'pool'}, dimensions={0} | all-to-all | bytes 131072 | tf_op jit(solution)/shard_map/all_to_all | solution.py:170
  235.0 89.2 %reduce-scatter.2.cloned.1.call-done = bf16[16,8192]{1,0:T(8,128)(2,1)} async-done(((bf16[512,8192]{1,0:T(8,128)(2,1)}), bf16[16,8192]{1,0:T(8,128)(2,1)}) %reduce-scatter.2.cloned.1.call-update) | async-done | bytes 262160 | tf_op jit(solution)/shard_map/reduce_scatter | solution.py:202
  324.2 1.8 convert_add_fusion
  (67 shorter events, 7.8 us)
Async XLA Ops:
  7.2 22.4 %copy-start = (bf16[512,1,2048]{2,0,1:T(8,128)(2,1)S(1)}, bf16[512,1,2048]{2,0,1:T(8,128)(2,1)}, u32[]{:S(2)}) copy-start(bf16[512,1,2048]{2,0,1:T(8,128)(2,1)} %param.15) | copy-start | bytes 6291460
  7.2 27.4 %copy-start.2 = (bf16[16,8192]{1,0:T(8,128)(2,1)S(1)}, bf16[16,8192]{1,0:T(8,128)(2,1)}, u32[]{:S(2)}) copy-start(bf16[16,8192]{1,0:T(8,128)(2,1)} %param.8) | copy-start | bytes 786436
  7.2 158.7 %all-gather.3.cloned.1.call-start = ((), (), s32[]{:S(2)}) async-start(), calls=%async_computation.5 | async-start | bytes 7077888 | tf_op jit(solution)/shard_map/all_gather | solution.py:36
  12.2 16.1 %all-to-all-start = ((s32[8,1,6]{2,1,0:T(1,128)}), s32[8,1,6]{2,1,0:T(1,128)S(1)}, u32[]{:S(2)}, u32[]{:S(2)}) async-start(s32[8,1,6]{2,1,0:T(1,128)} %bitcast), calls=%async_computation | async-start | bytes 8192 | tf_op jit(solution)/shard_map/all_to_all | solution.py:134
  31.2 18.1 %all-to-all-start.1 = ((bf16[8,6,2048]{2,1,0:T(8,128)(2,1)}), bf16[8,6,2048]{2,1,0:T(8,128)(2,1)S(1)}, u32[]{:S(2)}, u32[]{:S(2)}) async-start(bf16[8,6,2048]{2,1,0:T(8,128)(2,1)} %broadcast_select_fusion), calls=%async_computation.1 | async-start | bytes 524288 | tf_op jit(solution)/shard_map/all_to_all | solution.py:137
  53.5 8.6 %copy-start.4 = (s32[1,4]{1,0:T(1,128)S(1)}, s32[1,4]{1,0:T(1,128)}, u32[]{:S(2)}) copy-start(s32[1,4]{1,0:T(1,128)} %param.9) | copy-start | bytes 52
  53.5 9.0 %copy-start.3 = (s32[1024]{0:T(1024)S(1)}, s32[1024]{0:T(1024)}, u32[]{:S(2)}) copy-start(s32[1024]{0:T(1024)} %constant.140.clone.1) | copy-start | bytes 12292
  53.5 112.4 %all-to-all-start.2 = ((bf16[32,16,8192]{2,1,0:T(8,128)(2,1)}), bf16[32,16,8192]{2,1,0:T(8,128)(2,1)}, u32[]{:S(2)}, u32[]{:S(2)}) async-start(bf16[32,16,8192]{2,1,0:T(8,128)(2,1)} %stack.2), calls=%async_computation.2 | async-start | bytes 16777216 | tf_op jit(solution)/shard_map/all_to_all | solution.py:20
  61.3 152.7 %all-gather.5.cloned.1.call-start = ((), (), s32[]{:S(2)}) async-start(), calls=%async_computation.6 | async-start | bytes 4718592 | tf_op jit(solution)/shard_map/all_gather | solution.py:201
  62.0 262.1 %reduce-scatter.2.cloned.1.call-start = ((), (), s32[]{:S(2)}) async-start(), calls=%async_computation.7 | async-start | bytes 8650752 | tf_op jit(solution)/shard_map/reduce_scatter | solution.py:202
  64.0 1.3 collective-permute-start
  65.3 93.4 %collective-permute-start.1 = (bf16[2,512,64]{1,2,0:T(8,128)(2,1)S(1)}, bf16[2,512,64]{1,2,0:T(8,128)(2,1)S(1)}, u32[]{:S(2)}, u32[]{:S(2)}) collective-permute-start(bf16[2,512,64]{1,2,0:T(8,128)(2,1)S(1)} %maximum_select_fusion.2), channel_id=1, source_target_pairs={{0,2},{1,3},{2,0},{3,1},{4,6},{5,7},{6,4},{7,5},{8,10},{9,11},{10,... | collective-permute-start | bytes 393224 | tf_op jit(solution)/shard_map/ppermute | solution.py:42
  165.9 6.9 %copy-start.1 = (bf16[8192,320]{1,0:T(8,128)(2,1)S(1)}, bf16[8192,320]{1,0:T(8,128)(2,1)}, u32[]{:S(2)}) copy-start(bf16[8192,320]{1,0:T(8,128)(2,1)} %all-gather.3.cloned.1.call-done) | copy-start | bytes 15728644
  172.7 15.6 %collective-permute-start.2 = (bf16[1,512,64]{1,2,0:T(8,128)(2,1)S(1)}, bf16[1,512,64]{1,2,0:T(8,128)(2,1)S(1)}, u32[]{:S(2)}, u32[]{:S(2)}) collective-permute-start(bf16[1,512,64]{1,2,0:T(8,128)(2,1)S(1)} %fusion.13), channel_id=1, source_target_pairs={{0,1},{1,0},{2,3},{3,2},{4,5},{5,4},{6,7},{7,6},{8,9},{9,8},{10,11... | collective-permute-start | bytes 196616 | tf_op jit(solution)/shard_map/ppermute | solution.py:42
  188.4 16.1 %collective-permute-start.3 = (bf16[2,512,64]{1,2,0:T(8,128)(2,1)S(1)}, bf16[2,512,64]{1,2,0:T(8,128)(2,1)S(1)}, u32[]{:S(2)}, u32[]{:S(2)}) collective-permute-start(bf16[2,512,64]{1,2,0:T(8,128)(2,1)S(1)} %maximum_select_fusion.3), channel_id=1, source_target_pairs={{0,2},{1,3},{2,0},{3,1},{4,6},{5,7},{6,4},{7,5},{8,10},{9,11},{10,... | collective-permute-start | bytes 393224 | tf_op jit(solution)/shard_map/ppermute | solution.py:42
  221.7 0.7 copy-start.5
Sparse Core Ops, SparseCore 0:
  10.6 82.9 all-gather.2
  95.4 53.3 all-gather.4
  221.9 102.2 reduce-scatter.1
